TPU v7x, 32 devices: a whole 2x2x4 slice. The times are simulated.
32 devices in a mesh: dp: 16 (over z, y, core), fsdp: 2 (over x).
Axes of the slice: x: 2, y: 2, z: 4, core: 2. Of those that a mesh axis runs over, the one named last changes fastest.
Arguments:
- latents: bfloat16 [32768, 768], P(('dp', 'fsdp')), may hold values from -6 to 6
- size_tags: int32 [32], P(('dp', 'fsdp')), may hold values from 0 to 1
- timesteps: int32 [32, 4], P(('dp', 'fsdp')), may hold values from 0 to 999
- classes: int32 [32, 4], P(('dp', 'fsdp')), may hold values from 0 to 999
- step_table: bfloat16 [1000, 768], P('fsdp', 'dp'), may hold values from -5 to 5
- class_table: bfloat16 [1000, 768], P('fsdp', 'dp'), may hold values from -5 to 5
- modulation_weight: bfloat16 [768, 4608], P('fsdp', 'dp'), may hold values from -0.21875 to 0.21875
- attn_kernel: bfloat16 [9, 768], P(None, 'dp'), may hold values from -2 to 2
- qkv_weight: bfloat16 [768, 2304], P('fsdp', 'dp'), may hold values from -0.21875 to 0.21875
- proj_weight: bfloat16 [768, 768], P('fsdp', 'dp'), may hold values from -1.75 to 1.75
- expand_weight: bfloat16 [768, 3072], P('fsdp', 'dp'), may hold values from -0.21875 to 0.21875
- ffn_kernel: bfloat16 [9, 3072], P(None, 'dp'), may hold values from -2 to 2
- shrink_weight: bfloat16 [3072, 768], P('fsdp', 'dp'), may hold values from -0.109375 to 0.109375
- cotangent: bfloat16 [32768, 768], P(('dp', 'fsdp')), may hold values from -6 to 6
Outputs:
- block_output: bfloat16 [32768, 768], P(('dp', 'fsdp'))
- input_grad: float32 [32768, 768], P(('dp', 'fsdp'))
- step_table_grad: float32 [1000, 768], P('fsdp', 'dp')
- class_table_grad: float32 [1000, 768], P('fsdp', 'dp')
- modulation_grad: float32 [768, 4608], P('fsdp', 'dp')
- attn_kernel_grad: float32 [9, 768], P(None, 'dp')
- qkv_grad: float32 [768, 2304], P('fsdp', 'dp')
- proj_grad: float32 [768, 768], P('fsdp', 'dp')
- expand_grad: float32 [768, 3072], P('fsdp', 'dp')
- ffn_kernel_grad: float32 [9, 3072], P(None, 'dp')
- shrink_grad: float32 [3072, 768], P('fsdp', 'dp')
Inputs may be any that keep to these rules, and one draw needn't show every extreme that they name: `size_tags`: a slot with tag 0 holds one item of 1024 tokens, with tag 1 four items of 16 x 16 tokens. `timesteps`: in a slot with tag 0 only entry 0 is used. `classes`: in a slot with tag 0 only entry 0 is used.
All inputs are finite; a program needn't handle non-finite values.
Results may differ from a plain program's by a relative error of at most 0.019.
The roundings to bfloat16 on the way count: a program that leaves them out, or rounds other values in their place, can miss the bound.
Values may be sent and summed in bfloat16 or wider, within the bound.
No kernel may reach another device: no remote copies, remote signals or barrier semaphores. Data moves between devices by JAX's collectives and lax.ppermute only.
A program may use at most 384 MiB of HBM per device.

v0:
```python
import jax
import jax.numpy as jnp
from jax import lax
from jax.sharding import PartitionSpec as P

D = 768
H = 12
HD = 64
STEPS = 1000
CLASSES = 1000
SIDE = 32
GROUP = 256


def token_items(size_tag):
    row_index = jnp.arange(SIDE, dtype=jnp.int32)
    quadrant = row_index // (SIDE // 2)
    layout = quadrant[:, None] * 2 + quadrant[None, :]
    return (layout * size_tag).reshape(SIDE * SIDE)


def edge_masks(size_tag):
    row_index = jnp.arange(SIDE, dtype=jnp.int32)
    half_side = SIDE // 2
    collected = []
    for offset in (-1, 0, 1):
        neighbour = row_index + offset
        inside = (neighbour >= 0) & (neighbour < SIDE)
        same_item = jnp.maximum(neighbour, 0) // half_side == row_index // half_side
        collected.append((inside & (same_item | (size_tag == 0))).astype(jnp.float32))
    return collected


def depthwise(field, kernel, validity):
    channels = field.shape[-1]
    layout = field.reshape(SIDE, SIDE, channels)
    padded = jnp.pad(layout, ((1, 1), (1, 1), (0, 0)))
    summed = jnp.zeros_like(layout)
    for row_step in range(3):
        for col_step in range(3):
            window = padded[row_step : row_step + SIDE, col_step : col_step + SIDE]
            allowed = validity[row_step][:, None] * validity[col_step][None, :]
            summed = summed + window * allowed[:, :, None] * kernel[row_step * 3 + col_step]
    return summed.reshape(SIDE * SIDE, channels)


def to_groups(field):
    channels = field.shape[-1]
    layout = field.reshape(SIDE // 2, 2, SIDE // 2, 2, channels)
    return layout.transpose(1, 3, 0, 2, 4).reshape(4, GROUP, channels)


def from_groups(field):
    channels = field.shape[-1]
    layout = field.reshape(2, 2, SIDE // 2, SIDE // 2, channels)
    return layout.transpose(2, 0, 3, 1, 4).reshape(SIDE * SIDE, channels)


def same_item_mask(size_tag):
    position = jnp.arange(SIDE // 2, dtype=jnp.int32) // (SIDE // 4)
    labels = ((position[:, None] * 2 + position[None, :]) * size_tag).reshape(GROUP)
    return labels[:, None] == labels[None, :]


def normalize(values):
    centre = values - jnp.mean(values, axis=-1, keepdims=True)
    variance = jnp.mean(centre * centre, axis=-1, keepdims=True)
    return centre * lax.rsqrt(variance + 1e-06)


def modulate(values, offset_rows, scale_rows):
    return normalize(values) * (1.0 + scale_rows) + offset_rows


def per_token(mod_rows, labels):
    pieces = []
    for component in range(6):
        column = mod_rows[:, component * D : (component + 1) * D]
        chosen = column[0][None, :] * jnp.ones((labels.shape[0], 1), jnp.float32)
        for other_item in range(1, 4):
            chosen = jnp.where((labels == other_item)[:, None], column[other_item][None, :], chosen)
        pieces.append(chosen)
    return tuple(pieces)


def smooth_gate(values):
    return jax.nn.gelu(values, approximate=True)


def cross(left, right):
    return lax.dot_general(
        left, right, (((0,), (0,)), ((), ())), preferred_element_type=jnp.float32
    )


def against(left, right):
    return lax.dot_general(
        left, right, (((1,), (1,)), ((), ())), preferred_element_type=jnp.float32
    )


def attention_scores(queries, key_rows, allowed):
    scores = jnp.einsum(
        "gqhd,gkhd->ghqk", queries, key_rows, preferred_element_type=jnp.float32
    ) * HD ** (-0.5)
    return jnp.where(allowed[None, None], scores, -1e30)


def fetch_forward(
    step_table,
    class_table,
    modulation_weight,
    qkv_weight,
    proj_weight,
    expand_weight,
    shrink_weight,
    attn_kernel,
    ffn_kernel,
):
    gathered = (
        lax.all_gather(step_table, "fsdp", axis=0, tiled=True),
        lax.all_gather(class_table, "fsdp", axis=0, tiled=True),
        lax.all_gather(modulation_weight, "fsdp", axis=0, tiled=True),
        lax.all_gather(qkv_weight, "fsdp", axis=0, tiled=True),
        lax.all_gather(proj_weight, "fsdp", axis=0, tiled=True),
        lax.all_gather(expand_weight, "fsdp", axis=0, tiled=True),
        lax.all_gather(shrink_weight, "fsdp", axis=0, tiled=True),
    )
    return (
        lax.all_gather(gathered[0], "dp", axis=1, tiled=True),
        lax.all_gather(gathered[1], "dp", axis=1, tiled=True),
        lax.all_gather(gathered[2], "dp", axis=1, tiled=True),
        lax.all_gather(gathered[3], "dp", axis=1, tiled=True),
        lax.all_gather(gathered[4], "dp", axis=1, tiled=True),
        lax.all_gather(gathered[5], "dp", axis=1, tiled=True),
        lax.all_gather(gathered[6], "dp", axis=1, tiled=True),
        lax.all_gather(attn_kernel, "dp", axis=1, tiled=True),
        lax.all_gather(ffn_kernel, "dp", axis=1, tiled=True),
    )


def fetch_again(modulation_weight, qkv_weight, proj_weight, expand_weight, shrink_weight):
    gathered = (
        lax.all_gather(modulation_weight, "fsdp", axis=0, tiled=True),
        lax.all_gather(qkv_weight, "fsdp", axis=0, tiled=True),
        lax.all_gather(proj_weight, "fsdp", axis=0, tiled=True),
        lax.all_gather(expand_weight, "fsdp", axis=0, tiled=True),
        lax.all_gather(shrink_weight, "fsdp", axis=0, tiled=True),
    )
    return (
        lax.all_gather(gathered[0], "dp", axis=1, tiled=True),
        lax.all_gather(gathered[1], "dp", axis=1, tiled=True),
        lax.all_gather(gathered[2], "dp", axis=1, tiled=True),
        lax.all_gather(gathered[3], "dp", axis=1, tiled=True),
        lax.all_gather(gathered[4], "dp", axis=1, tiled=True),
    )


def body(
    latents,
    size_tags,
    timesteps,
    classes,
    step_table,
    class_table,
    modulation_weight,
    attn_kernel,
    qkv_weight,
    proj_weight,
    expand_weight,
    ffn_kernel,
    shrink_weight,
    cotangent,
):
    (
        step_full,
        class_full,
        mod_full,
        qkv_full,
        proj_full,
        expand_full,
        shrink_full,
        attn_full,
        ffn_full,
    ) = fetch_forward(
        step_table,
        class_table,
        modulation_weight,
        qkv_weight,
        proj_weight,
        expand_weight,
        shrink_weight,
        attn_kernel,
        ffn_kernel,
    )
    size_tag = size_tags[0]
    steps_hot = (timesteps[0][:, None] == jnp.arange(STEPS, dtype=jnp.int32)[None, :]).astype(
        jnp.float32
    )
    class_hot = (classes[0][:, None] == jnp.arange(CLASSES, dtype=jnp.int32)[None, :]).astype(
        jnp.float32
    )
    cond = jnp.dot(
        steps_hot.astype(jnp.bfloat16), step_full, preferred_element_type=jnp.float32
    ) + jnp.dot(class_hot.astype(jnp.bfloat16), class_full, preferred_element_type=jnp.float32)
    activated, silu_back = jax.vjp(jax.nn.silu, cond)
    act_low = activated.astype(jnp.bfloat16)
    mod_rows = jnp.dot(act_low, mod_full, preferred_element_type=jnp.float32)
    labels = token_items(size_tag)

    def spread_rows(rows):
        return per_token(rows, labels)

    (shift_one, scale_one, gate_one, shift_two, scale_two, gate_two), spread_back = jax.vjp(
        spread_rows, mod_rows
    )
    validity = edge_masks(size_tag)
    allowed = same_item_mask(size_tag)

    def conv_pass(field, kernel):
        return depthwise(field, kernel, validity)

    inputs = latents.astype(jnp.float32)
    first, first_back = jax.vjp(modulate, inputs, shift_one, scale_one)
    conv_out, conv_one_back = jax.vjp(conv_pass, first, attn_full.astype(jnp.float32))
    conv_low = conv_out.astype(jnp.bfloat16)
    qkv_low = jnp.dot(conv_low, qkv_full, preferred_element_type=jnp.float32).astype(jnp.bfloat16)
    grouped = to_groups(qkv_low).reshape(4, GROUP, 3, H, HD)
    queries = grouped[:, :, 0]
    key_rows = grouped[:, :, 1]
    value_rows = grouped[:, :, 2]
    scores = attention_scores(queries, key_rows, allowed)
    highest = jnp.max(scores, axis=-1, keepdims=True)
    raised = jnp.exp(scores - highest)
    totals = jnp.sum(raised, axis=-1, keepdims=True)
    probs_low = (raised / totals).astype(jnp.bfloat16)
    log_total = highest + jnp.log(totals)
    mixed = jnp.einsum("ghqk,gkhd->gqhd", probs_low, value_rows, preferred_element_type=jnp.float32)
    merged_low = from_groups(mixed.reshape(4, GROUP, D)).astype(jnp.bfloat16)
    attn = jnp.dot(merged_low, proj_full, preferred_element_type=jnp.float32)
    resid = inputs + gate_one * attn
    second, second_back = jax.vjp(modulate, resid, shift_two, scale_two)
    second_low = second.astype(jnp.bfloat16)
    expanded = jnp.dot(second_low, expand_full, preferred_element_type=jnp.float32)
    conved, conv_two_back = jax.vjp(conv_pass, expanded, ffn_full.astype(jnp.float32))
    hidden, gate_back = jax.vjp(smooth_gate, conved)
    hidden_low = hidden.astype(jnp.bfloat16)
    shrunk = jnp.dot(hidden_low, shrink_full, preferred_element_type=jnp.float32)
    block_output = (resid + gate_two * shrunk).astype(jnp.bfloat16)
    mod_back, qkv_back, proj_back, expand_back, shrink_back = fetch_again(
        modulation_weight, qkv_weight, proj_weight, expand_weight, shrink_weight
    )
    d_out = cotangent.astype(jnp.float32)
    d_gate_two = d_out * shrunk
    d_shrunk = (gate_two * d_out).astype(jnp.bfloat16)
    shrink_term = cross(hidden_low, d_shrunk)
    (d_conved,) = gate_back(against(d_shrunk, shrink_back))
    d_expanded, ffn_term = conv_two_back(d_conved)
    d_expanded_low = d_expanded.astype(jnp.bfloat16)
    expand_term = cross(second_low, d_expanded_low)
    d_resid_norm, d_shift_two, d_scale_two = second_back(against(d_expanded_low, expand_back))
    d_resid = d_out + d_resid_norm
    d_gate_one = d_resid * attn
    d_attn = (gate_one * d_resid).astype(jnp.bfloat16)
    proj_term = cross(merged_low, d_attn)
    d_merged = against(d_attn, proj_back).astype(jnp.bfloat16)
    d_mixed = to_groups(d_merged).reshape(4, GROUP, H, HD)
    probs_again = jnp.exp(attention_scores(queries, key_rows, allowed) - log_total)
    probs_again_low = probs_again.astype(jnp.bfloat16)
    d_values = jnp.einsum(
        "ghqk,gqhd->gkhd", probs_again_low, d_mixed, preferred_element_type=jnp.float32
    )
    d_probs = jnp.einsum("gqhd,gkhd->ghqk", d_mixed, value_rows, preferred_element_type=jnp.float32)
    inner = jnp.sum(probs_again * d_probs, axis=-1, keepdims=True)
    d_scores = (probs_again * (d_probs - inner)).astype(jnp.bfloat16)
    d_queries = jnp.einsum(
        "ghqk,gkhd->gqhd", d_scores, key_rows, preferred_element_type=jnp.float32
    ) * HD ** (-0.5)
    d_keys = jnp.einsum(
        "ghqk,gqhd->gkhd", d_scores, queries, preferred_element_type=jnp.float32
    ) * HD ** (-0.5)
    stacked = jnp.stack([d_queries, d_keys, d_values], axis=2).reshape(4, GROUP, 3 * D)
    d_qkv = from_groups(stacked).astype(jnp.bfloat16)
    qkv_term = cross(conv_low, d_qkv)
    d_first, attn_term = conv_one_back(against(d_qkv, qkv_back))
    d_input_norm, d_shift_one, d_scale_one = first_back(d_first)
    input_grad = d_resid + d_input_norm
    (d_mod,) = spread_back(
        (d_shift_one, d_scale_one, d_gate_one, d_shift_two, d_scale_two, d_gate_two)
    )
    d_mod_low = d_mod.astype(jnp.bfloat16)
    (d_cond,) = silu_back(against(d_mod_low, mod_back))
    mod_term = cross(act_low, d_mod_low)
    step_term = lax.dot_general(
        steps_hot, d_cond, (((0,), (0,)), ((), ())), precision=lax.Precision.HIGHEST
    )
    class_term = lax.dot_general(
        class_hot, d_cond, (((0,), (0,)), ((), ())), precision=lax.Precision.HIGHEST
    )
    (
        step_cols,
        class_cols,
        mod_cols_sum,
        qkv_cols,
        proj_cols,
        expand_cols,
        shrink_cols,
        attn_kernel_part,
        ffn_kernel_part,
    ) = (
        lax.psum_scatter(
            step_term.astype(jnp.bfloat16), "dp", scatter_dimension=1, tiled=True
        ).astype(jnp.float32),
        lax.psum_scatter(
            class_term.astype(jnp.bfloat16), "dp", scatter_dimension=1, tiled=True
        ).astype(jnp.float32),
        lax.psum_scatter(
            mod_term.astype(jnp.bfloat16), "dp", scatter_dimension=1, tiled=True
        ).astype(jnp.float32),
        lax.psum_scatter(
            qkv_term.astype(jnp.bfloat16), "dp", scatter_dimension=1, tiled=True
        ).astype(jnp.float32),
        lax.psum_scatter(
            proj_term.astype(jnp.bfloat16), "dp", scatter_dimension=1, tiled=True
        ).astype(jnp.float32),
        lax.psum_scatter(
            expand_term.astype(jnp.bfloat16), "dp", scatter_dimension=1, tiled=True
        ).astype(jnp.float32),
        lax.psum_scatter(
            shrink_term.astype(jnp.bfloat16), "dp", scatter_dimension=1, tiled=True
        ).astype(jnp.float32),
        lax.psum_scatter(
            attn_term.astype(jnp.bfloat16), "dp", scatter_dimension=1, tiled=True
        ).astype(jnp.float32),
        lax.psum_scatter(
            ffn_term.astype(jnp.bfloat16), "dp", scatter_dimension=1, tiled=True
        ).astype(jnp.float32),
    )
    step_grad, class_grad, mod_grad, qkv_grad, proj_grad, expand_grad, shrink_grad = (
        lax.psum_scatter(
            step_cols.astype(jnp.bfloat16), "fsdp", scatter_dimension=0, tiled=True
        ).astype(jnp.float32),
        lax.psum_scatter(
            class_cols.astype(jnp.bfloat16), "fsdp", scatter_dimension=0, tiled=True
        ).astype(jnp.float32),
        lax.psum_scatter(
            mod_cols_sum.astype(jnp.bfloat16), "fsdp", scatter_dimension=0, tiled=True
        ).astype(jnp.float32),
        lax.psum_scatter(
            qkv_cols.astype(jnp.bfloat16), "fsdp", scatter_dimension=0, tiled=True
        ).astype(jnp.float32),
        lax.psum_scatter(
            proj_cols.astype(jnp.bfloat16), "fsdp", scatter_dimension=0, tiled=True
        ).astype(jnp.float32),
        lax.psum_scatter(
            expand_cols.astype(jnp.bfloat16), "fsdp", scatter_dimension=0, tiled=True
        ).astype(jnp.float32),
        lax.psum_scatter(
            shrink_cols.astype(jnp.bfloat16), "fsdp", scatter_dimension=0, tiled=True
        ).astype(jnp.float32),
    )
    attn_kernel_grad, ffn_kernel_grad = lax.psum((attn_kernel_part, ffn_kernel_part), "fsdp")
    return (
        block_output,
        input_grad,
        step_grad,
        class_grad,
        mod_grad,
        attn_kernel_grad,
        qkv_grad,
        proj_grad,
        expand_grad,
        ffn_kernel_grad,
        shrink_grad,
    )


def solution(mesh):
    in_specs = (
        P(("dp", "fsdp"), None),
        P(("dp", "fsdp")),
        P(("dp", "fsdp"), None),
        P(("dp", "fsdp"), None),
        P("fsdp", "dp"),
        P("fsdp", "dp"),
        P("fsdp", "dp"),
        P(None, "dp"),
        P("fsdp", "dp"),
        P("fsdp", "dp"),
        P("fsdp", "dp"),
        P(None, "dp"),
        P("fsdp", "dp"),
        P(("dp", "fsdp"), None),
    )
    out_specs = (
        P(("dp", "fsdp"), None),
        P(("dp", "fsdp"), None),
        P("fsdp", "dp"),
        P("fsdp", "dp"),
        P("fsdp", "dp"),
        P(None, "dp"),
        P("fsdp", "dp"),
        P("fsdp", "dp"),
        P("fsdp", "dp"),
        P(None, "dp"),
        P("fsdp", "dp"),
    )
    return jax.shard_map(body, mesh=mesh, in_specs=in_specs, out_specs=out_specs, check_vma=False)
```

profile of v0, /device:TPU:0, one launch (start us, length us, event | category | flops | bytes accessed | tf_op | source)
XLA Modules:
  0.0 1364.5 jit_solution(2046139072494940579)
XLA Ops:
  56.5 21.9 %all-gather.2 = bf16[16,48,9]{1,2,0:T(8,128)(2,1)S(1)} all-gather(bf16[1,48,9]{1,2,0:T(8,128)(2,1)S(1)} %bitcast.230), channel_id=1, replica_groups=mesh['dp'=16,'fsdp'=2] {'dp'}, dimensions={0}, use_global_device_ids=true | all-gather | bytes 14688 | tf_op jit(solution)/shard_map/all_gather | solution.py:137
  78.7 17.9 %all-gather.3 = bf16[16,192,9]{1,2,0:T(8,128)(2,1)S(1)} all-gather(bf16[1,192,9]{1,2,0:T(8,128)(2,1)S(1)} %bitcast.229), channel_id=1, replica_groups=mesh['dp'=16,'fsdp'=2] {'dp'}, dimensions={0}, use_global_device_ids=true | all-gather | bytes 58752 | tf_op jit(solution)/shard_map/all_gather | solution.py:138
  101.4 63.7 %all-gather.16.cloned.1.call-done = bf16[768,4608]{0,1:T(8,128)(2,1)} async-done(((bf16[768,288]{0,1:T(8,128)(2,1)}), bf16[768,4608]{0,1:T(8,128)(2,1)}) %all-gather.16.cloned.1.call-update) | async-done | bytes 7077904 | tf_op jit(solution)/shard_map/all_gather | solution.py:132
  183.6 29.4 %all-gather.18.cloned.1.call-done = bf16[768,2304]{0,1:T(8,128)(2,1)} async-done(((bf16[768,144]{0,1:T(8,128)(2,1)}), bf16[768,2304]{0,1:T(8,128)(2,1)}) %all-gather.18.cloned.1.call-update) | async-done | bytes 3538960 | tf_op jit(solution)/shard_map/all_gather | solution.py:133
  235.8 14.9 %reshape_reshape.8 = bf16[4,256,3,12,64]{4,3,2,1,0:T(8,128)(2,1)} reshape(bf16[2,2,16,16,2304]{4,3,2,1,0:T(8,128)(2,1)} %bitcast.186) | data formatting | bytes 9437184 | tf_op jit(solution)/shard_map/reshape;reshape | solution.py:228
  321.5 22.1 %multiply_add_fusion = f32[32,32,3072]{2,1,0:T(8,128)} fusion(f32[32,32,3072]{2,1,0:T(8,128)S(1)} %bitcast.180, f32[3072]{0:T(1024)S(1)} %bitcast.200, f32[32,32]{1,0:T(8,128)S(1)} %get-tuple-element.159, f32[3072]{0:T(1024)S(1)} %bitcast.202, f32[32,32]{1,0:T(8,128)S(1)} %get-tuple-element.154, f32[3072]{0:T(1024)S(1)} %bitcast.204, ...), kind=kLoop, calls=%fused_computation.57 | loop fusion | flops 81788928 | bytes 25313280 | tf_op jit(solution)/shard_map/jvp()/add | solution.py:43
  361.3 63.2 %multiply_reduce_fusion.8 = (f32[3072]{0:T(1024)}, f32[3072]{0:T(1024)}, f32[3072]{0:T(1024)}, f32[3072]{0:T(1024)}, f32[3072]{0:T(1024)}, /*index=5*/f32[3072]{...) fusion(f32[32,32,3072]{2,1,0:T(8,128)} %bitcast.181, f32[32,32]{1,0:T(8,128)S(1)} %get-tuple-element.159, ...), kind=kOutput, calls=%fused_computation.44 | convolution fusion | flops 4971798528 | bytes 44186624 | tf_op jit(solution)/shard_map/dot_general | solution.py:97
  424.6 42.0 %multiply_multiply_fusion.10 = (f32[32,32,3072]{2,1,0:T(8,128)}, f32[32,32,3072]{2,1,0:T(8,128)}, f32[32,32,3072]{2,1,0:T(8,128)}, f32[32,32,3072]{2,1,0:T(8,128...) fusion(f32[32,32,3072]{2,1,0:T(8,128)} %bitcast.179, ...), kind=kLoop, calls=%fused_computation.56 | loop fusion | flops 56623104 | bytes 125976576 | tf_op jit(solution)/shard_map/transpose(jvp())/mul | solution.py:43
  466.6 23.6 %pad_add_fusion = f32[34,34,3072]{2,1,0:T(8,128)} fusion(f32[32,32,3072]{2,1,0:T(8,128)} %get-tuple-element.116, f32[32,32,3072]{2,1,0:T(8,128)} %get-tuple-element.117, f32[32,32,3072]{2,1,0:T(8,128)} %get-tuple-element.118, f32[32,32,3072]{2,1,0:T(8,128)} %get-tuple-element.110), kind=kLoop, calls=%fused_computation.10 | loop fusion | flops 10653696 | bytes 64536576 | tf_op jit(solution)/shard_map/transpose(jvp())/add_any | solution.py:41
  490.2 31.5 %fusion.14 = bf16[32,32,3072]{2,1,0:T(8,128)(2,1)} fusion(f32[32,32,3072]{2,1,0:T(8,128)} %get-tuple-element.111, f32[32,32,3072]{2,1,0:T(8,128)} %get-tuple-element.112, f32[32,32,3072]{2,1,0:T(8,128)} %get-tuple-element.113, f32[32,32,3072]{2,1,0:T(8,128)} %get-tuple-element.114, f32[32,32,3072]{2,1,0:T(8,128)} %get-tuple-element.115, ...), kind=kLoop, calls=%fused_computation.26 | loop fusion | flops 18874368 | bytes 81788928 | tf_op jit(solution)/shard_map/convert
  521.6 11.2 select_reduce_fusion.13
  533.0 12.0 fusion.86
  603.8 15.1 %copy.106 = bf16[4,256,3,12,64]{4,3,2,1,0:T(8,128)(2,1)} copy(bf16[4,256,3,12,64]{1,4,3,0,2:T(8,128)(2,1)} %maximum_convert_fusion) | data formatting | bytes 9437184 | tf_op jit(solution)/shard_map/convert_element_type | solution.py:283
  618.9 15.7 %convert_element_type.240 = bf16[2,2,16,16,2304]{4,3,2,1,0:T(8,128)(2,1)} reshape(bf16[4,256,3,12,64]{4,3,2,1,0:T(8,128)(2,1)} %copy.106) | data formatting | bytes 9437184 | tf_op jit(solution)/shard_map/convert_element_type | solution.py:283
  644.0 10.6 convert_element_type.242
  654.7 14.1 %multiply_multiply_fusion.19 = (f32[32,32,768]{2,1,0:T(8,128)}, f32[32,32,768]{2,1,0:T(8,128)S(1)}, f32[32,32,768]{2,1,0:T(8,128)S(1)}, f32[32,32,768]{2,1,0:T(8...) fusion(f32[768]{0:T(1024)S(1)} %copy-done.69, ...), kind=kOutput, calls=%fused_computation.160 | convolution fusion | flops 3638034432 | bytes 39779328 | tf_op jit(solution)/shard_map/dot_general | solution.py:97
  698.4 11.1 convert_element_type.252
  718.8 12.4 convolution_convert_fusion.3
  731.5 10.4 convolution_convert_fusion.2
  747.9 18.9 %multiply_reduce_fusion.18 = (f32[768]{0:T(1024)S(1)}, f32[768]{0:T(1024)S(1)}, f32[768]{0:T(1024)S(1)}, f32[768]{0:T(1024)S(1)}, f32[768]{0:T(1024)S(1)}, /*ind...) fusion(f32[32,32,768]{2,1,0:T(8,128)} %get-tuple-element.167, f32[32,32,768]{2,1,0:T(8,128)} %bitcast.183, ...), kind=kLoop, calls=%fused_computation.126 | loop fusion | flops 30663936 | bytes 7964672 | tf_op jit(solution)/shard_map/transpose(jvp())/reduce_sum | solution.py:43
  781.3 35.6 %reduce-scatter.29.cloned.1.call-done = bf16[1000,48]{0,1:T(8,128)(2,1)} async-done(((bf16[1000,768]{0,1:T(8,128)(2,1)}), bf16[1000,48]{0,1:T(8,128)(2,1)}) %reduce-scatter.29.cloned.1.call-update) | async-done | bytes 96016 | tf_op jit(solution)/shard_map/reduce_scatter | solution.py:311
  816.9 70.9 %reduce-scatter.35.cloned.1.call-done = bf16[768,144]{0,1:T(8,128)(2,1)} async-done(((bf16[768,2304]{0,1:T(8,128)(2,1)}), bf16[768,144]{0,1:T(8,128)(2,1)}) %reduce-scatter.35.cloned.1.call-update) | async-done | bytes 221200 | tf_op jit(solution)/shard_map/reduce_scatter | solution.py:320
  889.7 76.3 %reduce-scatter.39.cloned.1.call-done = bf16[768,192]{0,1:T(8,128)(2,1)} async-done(((bf16[768,3072]{0,1:T(8,128)(2,1)}), bf16[768,192]{0,1:T(8,128)(2,1)}) %reduce-scatter.39.cloned.1.call-update) | async-done | bytes 294928 | tf_op jit(solution)/shard_map/reduce_scatter | solution.py:326
  969.3 75.8 %reduce-scatter.41.cloned.1.call-done = bf16[3072,48]{0,1:T(8,128)(2,1)} async-done(((bf16[3072,768]{0,1:T(8,128)(2,1)}), bf16[3072,48]{0,1:T(8,128)(2,1)}) %reduce-scatter.41.cloned.1.call-update) | async-done | bytes 294928 | tf_op jit(solution)/shard_map/reduce_scatter | solution.py:329
  1050.6 87.5 %reduce-scatter.33.cloned.1.call-done = bf16[768,288]{0,1:T(8,128)(2,1)} async-done(((bf16[768,4608]{0,1:T(8,128)(2,1)}), bf16[768,288]{0,1:T(8,128)(2,1)}) %reduce-scatter.33.cloned.1.call-update) | async-done | bytes 442384 | tf_op jit(solution)/shard_map/reduce_scatter | solution.py:317
  1145.3 50.3 %reduce-scatter.47.cloned.1.call-done = bf16[48,9]{1,0:T(8,128)(2,1)} async-done(((bf16[768,9]{1,0:T(8,128)(2,1)}), bf16[48,9]{1,0:T(8,128)(2,1)}) %reduce-scatter.47.cloned.1.call-update) | async-done | bytes 880
  1196.3 58.7 %reduce-scatter.55.cloned.1.call-done = bf16[192,9]{1,0:T(8,128)(2,1)} async-done(((bf16[3072,9]{1,0:T(8,128)(2,1)}), bf16[192,9]{1,0:T(8,128)(2,1)}) %reduce-scatter.55.cloned.1.call-update) | async-done | bytes 3472
  1269.3 23.1 %all-reduce.74.cloned.1.call-done = (bf16[1000,48]{0,1:T(8,128)(2,1)}, bf16[1000,48]{0,1:T(8,128)(2,1)}) async-done(((bf16[1000,48]{0,1:T(8,128)(2,1)}, bf16[1000,48]{0,1:T(8,128)(2,1)}), (bf16[1000,48]{0,1:T(8,128)(2,1)}, bf16[1000,48]{0,1:T(8,128)(2,1)})) %all-reduce.74.cloned.1.call-update) | async-done | bytes 192016
  1295.4 12.9 reduce-scatter.49.cloned.1.call-done
  1310.1 13.6 reduce-scatter.53.cloned.1.call-done
  1325.4 12.5 reduce-scatter.43.cloned.1.call-done
  1339.6 15.9 %reduce-scatter.45.cloned.1.call-done = bf16[384,288]{1,0:T(8,128)(2,1)} async-done(((bf16[768,288]{1,0:T(8,128)(2,1)}), bf16[384,288]{1,0:T(8,128)(2,1)}) %reduce-scatter.45.cloned.1.call-update) | async-done | bytes 221200
  (481 shorter events, 351.6 us)
Async XLA Ops:
  7.2 90.3 %all-gather.12.cloned.1.call-start = ((), (), s32[]{:S(2)}) async-start(), calls=%async_computation.14 | async-start | bytes 1671168 | tf_op jit(solution)/shard_map/all_gather | solution.py:130
  14.2 85.3 %all-gather.14.cloned.1.call-start = ((), (), s32[]{:S(2)}) async-start(), calls=%async_computation.15 | async-start | bytes 1671168 | tf_op jit(solution)/shard_map/all_gather | solution.py:131
  20.1 145.0 %all-gather.16.cloned.1.call-start = ((), (), s32[]{:S(2)}) async-start(), calls=%async_computation.16 | async-start | bytes 7520256 | tf_op jit(solution)/shard_map/all_gather | solution.py:132
  28.7 184.3 %all-gather.18.cloned.1.call-start = ((), (), s32[]{:S(2)}) async-start(), calls=%async_computation.17 | async-start | bytes 3760128 | tf_op jit(solution)/shard_map/all_gather | solution.py:133
  34.5 269.0 %all-gather.20.cloned.1.call-start = ((), (), s32[]{:S(2)}) async-start(), calls=%async_computation.18 | async-start | bytes 1253376 | tf_op jit(solution)/shard_map/all_gather | solution.py:134
  41.1 270.6 %all-gather.22.cloned.1.call-start = ((), (), s32[]{:S(2)}) async-start(), calls=%async_computation.19 | async-start | bytes 5013504 | tf_op jit(solution)/shard_map/all_gather | solution.py:135
  47.7 313.6 %all-gather.24.cloned.1.call-start = ((), (), s32[]{:S(2)}) async-start(), calls=%async_computation.20 | async-start | bytes 5013504 | tf_op jit(solution)/shard_map/all_gather | solution.py:136
  53.7 725.7 %reduce-scatter.37.cloned.1.call-start = ((), (), s32[]{:S(2)}) async-start(), calls=%async_computation.25 | async-start | bytes 1253376 | tf_op jit(solution)/shard_map/reduce_scatter | solution.py:323
  54.8 116.7 %copy-start.26 = (f32[1024]{0:T(1024)}, f32[1024]{0:T(1024)S(1)}, u32[]{:S(2)}) copy-start(f32[1024]{0:T(1024)S(1)} %broadcast_multiply_fusion.10) | copy-start | bytes 12292
  55.4 116.1 %copy-start.32 = (f32[1024]{0:T(1024)}, f32[1024]{0:T(1024)S(1)}, u32[]{:S(2)}) copy-start(f32[1024]{0:T(1024)S(1)} %fusion.71) | copy-start | bytes 12292
  55.7 109.5 %copy-start.84 = (pred[32,32]{1,0:T(8,128)(4,1)}, pred[32,32]{1,0:T(8,128)(4,1)S(1)}, u32[]{:S(2)}) copy-start(pred[32,32]{1,0:T(8,128)(4,1)S(1)} %get-tuple-element.150) | copy-start | bytes 3076
  56.3 115.2 %copy-start.42 = (pred[1024]{0:T(1024)(128)(4,1)}, pred[1024]{0:T(1024)(128)(4,1)S(1)}, u32[]{:S(2)}) copy-start(pred[1024]{0:T(1024)(128)(4,1)S(1)} %eq.146) | copy-start | bytes 3076
  56.4 115.2 %copy-start.45 = (pred[1024]{0:T(1024)(128)(4,1)}, pred[1024]{0:T(1024)(128)(4,1)S(1)}, u32[]{:S(2)}) copy-start(pred[1024]{0:T(1024)(128)(4,1)S(1)} %eq.144) | copy-start | bytes 3076
  56.5 225.7 %copy-start.17 = (pred[256,256]{0,1:T(8,128)(4,1)}, pred[256,256]{0,1:T(8,128)(4,1)S(1)}, u32[]{:S(2)}) copy-start(pred[256,256]{0,1:T(8,128)(4,1)S(1)} %broadcast_compare_fusion) | copy-start | bytes 196612
  309.0 223.9 %copy-start.97 = (f32[1024]{0:T(1024)}, f32[1024]{0:T(1024)S(1)}, u32[]{:S(2)}) copy-start(f32[1024]{0:T(1024)S(1)} %broadcast_multiply_fusion.9) | copy-start | bytes 12292
  311.1 221.8 %copy-start.123 = (f32[1024]{0:T(1024)}, f32[1024]{0:T(1024)S(1)}, u32[]{:S(2)}) copy-start(f32[1024]{0:T(1024)S(1)} %fusion.72) | copy-start | bytes 12292
  599.8 181.5 %reduce-scatter.31.cloned.1.call-start = ((), (), s32[]{:S(2)}) async-start(), calls=%async_computation.22 | async-start | bytes 1671168 | tf_op jit(solution)/shard_map/reduce_scatter | solution.py:314
  695.6 121.2 %reduce-scatter.29.cloned.1.call-start = ((), (), s32[]{:S(2)}) async-start(), calls=%async_computation.21 | async-start | bytes 1671168 | tf_op jit(solution)/shard_map/reduce_scatter | solution.py:311
  698.4 189.5 %reduce-scatter.35.cloned.1.call-start = ((), (), s32[]{:S(2)}) async-start(), calls=%async_computation.24 | async-start | bytes 3760128 | tf_op jit(solution)/shard_map/reduce_scatter | solution.py:320
  718.2 247.9 %reduce-scatter.39.cloned.1.call-start = ((), (), s32[]{:S(2)}) async-start(), calls=%async_computation.26 | async-start | bytes 5013504 | tf_op jit(solution)/shard_map/reduce_scatter | solution.py:326
  731.3 313.8 %reduce-scatter.41.cloned.1.call-start = ((), (), s32[]{:S(2)}) async-start(), calls=%async_computation.27 | async-start | bytes 5013504 | tf_op jit(solution)/shard_map/reduce_scatter | solution.py:329
  741.9 396.1 %reduce-scatter.33.cloned.1.call-start = ((), (), s32[]{:S(2)}) async-start(), calls=%async_computation.23 | async-start | bytes 7520256 | tf_op jit(solution)/shard_map/reduce_scatter | solution.py:317
  747.0 448.5 %reduce-scatter.47.cloned.1.call-start = ((), (), s32[]{:S(2)}) async-start(), calls=%async_computation.30 | async-start | bytes 208896
  777.8 190.2 %copy-start.129 = (u32[32]{0:T(128)S(1)}, u32[32]{0:T(128)}, u32[]{:S(2)}) copy-start(u32[32]{0:T(128)} %constant.323) | copy-start | bytes 388
  777.8 267.6 %copy-start.65 = (f32[1024]{0:T(1024)S(1)}, f32[1024]{0:T(1024)}, u32[]{:S(2)}) copy-start(f32[1024]{0:T(1024)} %copy-done.64) | copy-start | bytes 12292
  777.8 477.2 %reduce-scatter.55.cloned.1.call-start = ((), (), s32[]{:S(2)}) async-start(), calls=%async_computation.34 | async-start | bytes 835584
  779.4 488.2 %reduce-scatter.51.cloned.1.call-start = ((), (), s32[]{:S(2)}) async-start(), calls=%async_computation.32 | async-start | bytes 294912
  781.2 511.1 %all-reduce.74.cloned.1.call-start = ((), (), s32[]{:S(2)}) async-start(), calls=%async_computation.35 | async-start | bytes 393216
  816.9 491.4 %reduce-scatter.49.cloned.1.call-start = ((), (), s32[]{:S(2)}) async-start(), calls=%async_computation.31 | async-start | bytes 589824
  889.7 433.9 %reduce-scatter.53.cloned.1.call-start = ((), (), s32[]{:S(2)}) async-start(), calls=%async_computation.33 | async-start | bytes 589824
  968.0 370.0 %reduce-scatter.43.cloned.1.call-start = ((), (), s32[]{:S(2)}) async-start(), calls=%async_computation.28 | async-start | bytes 442368 | tf_op jit(solution)/shard_map/reduce_scatter | solution.py:358
  1045.1 310.4 %reduce-scatter.45.cloned.1.call-start = ((), (), s32[]{:S(2)}) async-start(), calls=%async_computation.29 | async-start | bytes 884736
  (125 other events, 2171.6 us)
Sparse Core Ops, SparseCore 0:
  14.3 41.3 all-gather.11
  58.6 38.7 all-gather.13
  99.7 65.4 all-gather.15
  167.3 45.6 all-gather.17
  215.1 37.3 all-gather.19
  254.6 52.3 all-gather.21
  309.3 51.9 all-gather.23
  599.9 56.6 reduce-scatter.36
  695.7 58.0 reduce-scatter.30
  758.3 58.4 reduce-scatter.28
  820.7 67.0 reduce-scatter.34
  891.5 74.4 reduce-scatter.38
  970.4 74.6 reduce-scatter.40
  1048.9 89.0 reduce-scatter.32
  1142.4 53.0 reduce-scatter.46
  1199.3 55.5 reduce-scatter.54
  1257.6 9.9 reduce-scatter.50
  1269.8 22.4 all-reduce.73
  1295.1 13.1 reduce-scatter.48
  1310.5 13.1 reduce-scatter.52
  1325.9 12.0 reduce-scatter.42
  1340.2 15.2 reduce-scatter.44
where the time goes:
time: 1380 us; the launch traced here: 1360 us
  waiting for transfers between devices  637 us (46%)
  other arithmetic  229 us (17%)
  matrix products  210 us (15%)
  local copies, waits for them, and re-layouts  176 us (13%)
  blocking collectives  92.9 us (7%)
  between operations  18.2 us (1%)
    unnamed x29, waiting for transfers between devices  178 us
    dot_general x5, matrix products, against(): lax.dot_general(left, right, (((1,), (1,)), ((), ())), preferred_element_...  93.4 us
    reduce_scatter x1, waiting for transfers between devices, body(): lax.psum_scatter(mod_term.astype(jnp.bfloat16), 'dp', scatter_dimension=1...  87.5 us
    reduce_scatter x1, waiting for transfers between devices, body(): lax.psum_scatter(expand_term.astype(jnp.bfloat16), 'dp', scatter_dimensio...  76.3 us
    reduce_scatter x1, waiting for transfers between devices, body(): lax.psum_scatter(shrink_term.astype(jnp.bfloat16), 'dp', scatter_dimensio...  75.8 us
    reduce_scatter x1, waiting for transfers between devices, body(): lax.psum_scatter(qkv_term.astype(jnp.bfloat16), 'dp', scatter_dimension=1...  70.9 us
    all_gather x1, waiting for transfers between devices, fetch_forward(): lax.all_gather(gathered[2], 'dp', axis=1, tiled=True)  63.7 us
    convert_element_type x5, local copies, waits for them, and re-layouts, body(): d_qkv = from_groups(stacked).astype(jnp.bfloat16)  61.8 us
  transfers between devices with their start and end apart: 22, of which 16 were waited for; matrix products, arithmetic and copies ran while one was open for 27% of the time, Pallas kernels for 0%

commit v1 on v0

--- a/solution.py
+++ b/solution.py
@@ -2,6 +2,7 @@
 import jax.numpy as jnp
 from jax import lax
 from jax.sharding import PartitionSpec as P
+from jax.lax import axis_index, ppermute, psum
 
 D = 768
 H = 12
@@ -10,6 +11,26 @@
 CLASSES = 1000
 SIDE = 32
 GROUP = 256
+
+
+def match_side(s0):
+    total_devices = psum(1, "dp")
+    u_next = range(total_devices)
+    b_now = map(lambda dev_j: (dev_j, (dev_j + 1) % total_devices), u_next)
+    pieces_in = list(b_now)
+    u1 = range(total_devices)
+    value_now = map(lambda dev_j: (dev_j, (dev_j - 1) % total_devices), u1)
+    tray = list(value_now)
+    row_out, arr_now = ([s0], [s0])
+    for _ in range(total_devices // 2):
+        block_last = ppermute(row_out[-1], "dp", pieces_in)
+        row_out.append(block_last)
+    for _ in [*range((total_devices - 1) // 2)]:
+        mixed_arr = ppermute(arr_now[-1], "dp", tray)
+        arr_now.append(mixed_arr)
+    upper = jnp.concatenate([*row_out[::-1], *arr_now[1:]], axis=1)
+    found_now = axis_index("dp")
+    return jnp.roll(upper, (found_now - total_devices // 2) * s0.shape[1], axis=1)
 
 
 def token_items(size_tag):
@@ -129,7 +150,7 @@
     return (
         lax.all_gather(gathered[0], "dp", axis=1, tiled=True),
         lax.all_gather(gathered[1], "dp", axis=1, tiled=True),
-        lax.all_gather(gathered[2], "dp", axis=1, tiled=True),
+        match_side(gathered[2]),
         lax.all_gather(gathered[3], "dp", axis=1, tiled=True),
         lax.all_gather(gathered[4], "dp", axis=1, tiled=True),
         lax.all_gather(gathered[5], "dp", axis=1, tiled=True),

time: 1380 us -> 1360 us (0.986)
  waiting for transfers between devices: 637 us -> 543 us
  starting transfers between devices: 1.29 us -> 53.3 us
  local copies, waits for them, and re-layouts: 176 us -> 198 us
    reduce_scatter x1, waiting for transfers between devices: 70.9 us -> 0.02 us  [body(): lax.psum_scatter(qkv_term.astype(jnp.bfloat16), 'dp', scatter_dimension=1...]
    all_gather x1, waiting for transfers between devices: 63.7 us -> 0.02 us  [fetch_again(): lax.all_gather(gathered[0], 'dp', axis=1, tiled=True)]
    ppermute x0 -> x15, starting transfers between devices: none -> 51.9 us  [the longest x8 29.1 us: match_side(): block_last = ppermute(row_out[-1], 'dp', pieces_in)]
    all_gather x1, waiting for transfers between devices: 29.4 us -> 0.02 us  [fetch_forward(): lax.all_gather(gathered[3], 'dp', axis=1, tiled=True)]
    ppermute x0 -> x15, waiting for transfers between devices: none -> 28.4 us  [the longest x8 23.8 us: match_side(): block_last = ppermute(row_out[-1], 'dp', pieces_in)]
    reduce_scatter x1, waiting for transfers between devices: 35.6 us -> 63.3 us  [body(): lax.psum_scatter(step_term.astype(jnp.bfloat16), 'dp', scatter_dimension=...]
    unnamed x288 -> x321, local copies, waits for them, and re-layouts: 40.3 us -> 62.2 us
    reduce_scatter x1, waiting for transfers between devices: 0.02 us -> 19.9 us  [body(): lax.psum_scatter(class_term.astype(jnp.bfloat16), 'dp', scatter_dimension...]
  transfers between devices with their start and end apart: 22 -> 37, of which waited for: 16 -> 22; matrix products, arithmetic and copies ran while one was open for 27% -> 46% of each run, Pallas kernels for 0% -> 0%
where the time goes in v1:
time: 1360 us; the launch traced here: 1350 us
  waiting for transfers between devices  543 us (40%)
  other arithmetic  227 us (17%)
  matrix products  214 us (16%)
  local copies, waits for them, and re-layouts  198 us (15%)
  blocking collectives  97.1 us (7%)
  starting transfers between devices  53.3 us (4%)
  between operations  18.4 us (1%)
    unnamed x29, waiting for transfers between devices  178 us
    dot_general x5, matrix products, against(): lax.dot_general(left, right, (((1,), (1,)), ((), ())), preferred_element_...  96 us
    reduce_scatter x1, waiting for transfers between devices, body(): lax.psum_scatter(mod_term.astype(jnp.bfloat16), 'dp', scatter_dimension=1...  87.5 us
    reduce_scatter x1, waiting for transfers between devices, body(): lax.psum_scatter(expand_term.astype(jnp.bfloat16), 'dp', scatter_dimensio...  78.2 us
    reduce_scatter x1, waiting for transfers between devices, body(): lax.psum_scatter(shrink_term.astype(jnp.bfloat16), 'dp', scatter_dimensio...  75.7 us
    reduce_scatter x1, waiting for transfers between devices, body(): lax.psum_scatter(step_term.astype(jnp.bfloat16), 'dp', scatter_dimension=...  63.3 us
    unnamed x321, local copies, waits for them, and re-layouts  62.2 us
    convert_element_type x5, local copies, waits for them, and re-layouts, body(): d_qkv = from_groups(stacked).astype(jnp.bfloat16)  61.5 us
  transfers between devices with their start and end apart: 37, of which 22 were waited for; matrix products, arithmetic and copies ran while one was open for 46% of the time, Pallas kernels for 0%

profile of v1, /device:TPU:0, one launch (start us, length us, event | category | flops | bytes accessed | tf_op | source)
XLA Modules:
  0.0 1351.5 jit_solution(1656992339171687182)
XLA Ops:
  56.5 22.1 %all-gather.2 = bf16[16,48,9]{1,2,0:T(8,128)(2,1)S(1)} all-gather(bf16[1,48,9]{1,2,0:T(8,128)(2,1)S(1)} %bitcast.227), channel_id=1, replica_groups=mesh['dp'=16,'fsdp'=2] {'dp'}, dimensions={0}, use_global_device_ids=true | all-gather | bytes 14688 | tf_op jit(solution)/shard_map/all_gather | solution.py:158
  78.8 20.5 %all-gather.3 = bf16[16,192,9]{1,2,0:T(8,128)(2,1)S(1)} all-gather(bf16[1,192,9]{1,2,0:T(8,128)(2,1)S(1)} %bitcast.226), channel_id=1, replica_groups=mesh['dp'=16,'fsdp'=2] {'dp'}, dimensions={0}, use_global_device_ids=true | all-gather | bytes 58752 | tf_op jit(solution)/shard_map/all_gather | solution.py:159
  139.0 10.3 collective-permute-start.4
  228.1 10.3 reshape.849
  243.5 15.0 %reshape_reshape.8 = bf16[4,256,3,12,64]{4,3,2,1,0:T(8,128)(2,1)} reshape(bf16[2,2,16,16,2304]{4,3,2,1,0:T(8,128)(2,1)} %bitcast.183) | data formatting | bytes 9437184 | tf_op jit(solution)/shard_map/reshape;reshape | solution.py:249
  333.2 22.2 %multiply_add_fusion = f32[32,32,3072]{2,1,0:T(8,128)} fusion(f32[32,32,3072]{2,1,0:T(8,128)S(1)} %bitcast.177, f32[3072]{0:T(1024)S(1)} %bitcast.197, f32[32,32]{1,0:T(8,128)S(1)} %get-tuple-element.159, f32[3072]{0:T(1024)S(1)} %bitcast.199, f32[32,32]{1,0:T(8,128)S(1)} %get-tuple-element.154, f32[3072]{0:T(1024)S(1)} %bitcast.201, ...), kind=kLoop, calls=%fused_computation.57 | loop fusion | flops 81788928 | bytes 25313280 | tf_op jit(solution)/shard_map/jvp()/add | solution.py:64
  355.4 63.3 %multiply_reduce_fusion.8 = (f32[3072]{0:T(1024)}, f32[3072]{0:T(1024)}, f32[3072]{0:T(1024)}, f32[3072]{0:T(1024)}, f32[3072]{0:T(1024)}, /*index=5*/f32[3072]{...) fusion(f32[32,32,3072]{2,1,0:T(8,128)} %bitcast.178, f32[32,32]{1,0:T(8,128)S(1)} %get-tuple-element.159, ...), kind=kOutput, calls=%fused_computation.44 | convolution fusion | flops 4971798528 | bytes 44186624 | tf_op jit(solution)/shard_map/dot_general | solution.py:118
  418.7 42.0 %multiply_multiply_fusion.10 = (f32[32,32,3072]{2,1,0:T(8,128)}, f32[32,32,3072]{2,1,0:T(8,128)}, f32[32,32,3072]{2,1,0:T(8,128)}, f32[32,32,3072]{2,1,0:T(8,128...) fusion(f32[32,32,3072]{2,1,0:T(8,128)} %bitcast.176, ...), kind=kLoop, calls=%fused_computation.56 | loop fusion | flops 56623104 | bytes 125976576 | tf_op jit(solution)/shard_map/transpose(jvp())/mul | solution.py:64
  460.8 23.6 %pad_add_fusion = f32[34,34,3072]{2,1,0:T(8,128)} fusion(f32[32,32,3072]{2,1,0:T(8,128)} %get-tuple-element.116, f32[32,32,3072]{2,1,0:T(8,128)} %get-tuple-element.117, f32[32,32,3072]{2,1,0:T(8,128)} %get-tuple-element.118, f32[32,32,3072]{2,1,0:T(8,128)} %get-tuple-element.110), kind=kLoop, calls=%fused_computation.10 | loop fusion | flops 10653696 | bytes 64536576 | tf_op jit(solution)/shard_map/transpose(jvp())/add_any | solution.py:62
  484.3 31.7 %fusion.14 = bf16[32,32,3072]{2,1,0:T(8,128)(2,1)} fusion(f32[32,32,3072]{2,1,0:T(8,128)} %get-tuple-element.111, f32[32,32,3072]{2,1,0:T(8,128)} %get-tuple-element.112, f32[32,32,3072]{2,1,0:T(8,128)} %get-tuple-element.113, f32[32,32,3072]{2,1,0:T(8,128)} %get-tuple-element.114, f32[32,32,3072]{2,1,0:T(8,128)} %get-tuple-element.115, ...), kind=kLoop, calls=%fused_computation.26 | loop fusion | flops 18874368 | bytes 81788928 | tf_op jit(solution)/shard_map/convert
  516.0 12.3 select_reduce_fusion.13
  533.2 13.6 %fusion.88 = (f32[1024]{0:T(1024)S(1)}, f32[1024,768]{1,0:T(8,128)S(1)}, f32[1024,768]{1,0:T(8,128)}, bf16[1024,768]{1,0:T(8,128)(2,1)}, f32[1024,768]{1,0:T(8,128)}) fusion(f32[1024]{0:T(1024)S(1)} %multiply_multiply_fusion.22, f32[1024,768]{1,0:T(8,128)S(1)} %copy-done.19, f32[1024]{0:T(1024)S(1)} %broadcast_multiply_fusion.9, f32[1024]{0:T(1024)S(1)} %fusion.74, ...), kind=kOutput, calls=%fused_computation.340 | convolution fusion | flops 4846779392 | bytes 28355584 | tf_op jit(solution)/shard_map/dot_general | solution.py:269
  609.6 15.0 %copy.106 = bf16[4,256,3,12,64]{4,3,2,1,0:T(8,128)(2,1)} copy(bf16[4,256,3,12,64]{1,4,3,0,2:T(8,128)(2,1)} %maximum_convert_fusion) | data formatting | bytes 9437184 | tf_op jit(solution)/shard_map/convert_element_type | solution.py:304
  624.7 15.6 %convert_element_type.240 = bf16[2,2,16,16,2304]{4,3,2,1,0:T(8,128)(2,1)} reshape(bf16[4,256,3,12,64]{4,3,2,1,0:T(8,128)(2,1)} %copy.106) | data formatting | bytes 9437184 | tf_op jit(solution)/shard_map/convert_element_type | solution.py:304
  649.7 10.6 convert_element_type.252
  660.3 10.8 convert_element_type.242
  681.2 13.7 %multiply_multiply_fusion.19 = (f32[32,32,768]{2,1,0:T(8,128)}, f32[32,32,768]{2,1,0:T(8,128)S(1)}, f32[32,32,768]{2,1,0:T(8,128)S(1)}, f32[32,32,768]{2,1,0:T(8...) fusion(f32[768]{0:T(1024)S(1)} %copy-done.73, ...), kind=kOutput, calls=%fused_computation.162 | convolution fusion | flops 3638034432 | bytes 39779328 | tf_op jit(solution)/shard_map/dot_general | solution.py:118
  726.7 12.3 convolution_convert_fusion.3
  739.7 10.4 convolution_convert_fusion.2
  756.0 19.1 %multiply_reduce_fusion.18 = (f32[768]{0:T(1024)S(1)}, f32[768]{0:T(1024)S(1)}, f32[768]{0:T(1024)S(1)}, f32[768]{0:T(1024)S(1)}, f32[768]{0:T(1024)S(1)}, /*ind...) fusion(f32[32,32,768]{2,1,0:T(8,128)} %get-tuple-element.167, f32[32,32,768]{2,1,0:T(8,128)} %bitcast.182, ...), kind=kLoop, calls=%fused_computation.128 | loop fusion | flops 30663936 | bytes 7964672 | tf_op jit(solution)/shard_map/transpose(jvp())/reduce_sum | solution.py:64
  791.3 19.9 %reduce-scatter.31.cloned.1.call-done = bf16[1000,48]{0,1:T(8,128)(2,1)} async-done(((bf16[1000,768]{0,1:T(8,128)(2,1)}), bf16[1000,48]{0,1:T(8,128)(2,1)}) %reduce-scatter.31.cloned.1.call-update) | async-done | bytes 96016 | tf_op jit(solution)/shard_map/reduce_scatter | solution.py:335
  811.2 63.3 %reduce-scatter.29.cloned.1.call-done = bf16[1000,48]{0,1:T(8,128)(2,1)} async-done(((bf16[1000,768]{0,1:T(8,128)(2,1)}), bf16[1000,48]{0,1:T(8,128)(2,1)}) %reduce-scatter.29.cloned.1.call-update) | async-done | bytes 96016 | tf_op jit(solution)/shard_map/reduce_scatter | solution.py:332
  874.6 78.2 %reduce-scatter.39.cloned.1.call-done = bf16[768,192]{0,1:T(8,128)(2,1)} async-done(((bf16[768,3072]{0,1:T(8,128)(2,1)}), bf16[768,192]{0,1:T(8,128)(2,1)}) %reduce-scatter.39.cloned.1.call-update) | async-done | bytes 294928 | tf_op jit(solution)/shard_map/reduce_scatter | solution.py:347
  956.0 75.7 %reduce-scatter.41.cloned.1.call-done = bf16[3072,48]{0,1:T(8,128)(2,1)} async-done(((bf16[3072,768]{0,1:T(8,128)(2,1)}), bf16[3072,48]{0,1:T(8,128)(2,1)}) %reduce-scatter.41.cloned.1.call-update) | async-done | bytes 294928 | tf_op jit(solution)/shard_map/reduce_scatter | solution.py:350
  1037.3 87.5 %reduce-scatter.33.cloned.1.call-done = bf16[768,288]{0,1:T(8,128)(2,1)} async-done(((bf16[768,4608]{0,1:T(8,128)(2,1)}), bf16[768,288]{0,1:T(8,128)(2,1)}) %reduce-scatter.33.cloned.1.call-update) | async-done | bytes 442384 | tf_op jit(solution)/shard_map/reduce_scatter | solution.py:338
  1132.0 50.3 %reduce-scatter.47.cloned.1.call-done = bf16[48,9]{1,0:T(8,128)(2,1)} async-done(((bf16[768,9]{1,0:T(8,128)(2,1)}), bf16[48,9]{1,0:T(8,128)(2,1)}) %reduce-scatter.47.cloned.1.call-update) | async-done | bytes 880
  1183.1 58.7 %reduce-scatter.55.cloned.1.call-done = bf16[192,9]{1,0:T(8,128)(2,1)} async-done(((bf16[3072,9]{1,0:T(8,128)(2,1)}), bf16[192,9]{1,0:T(8,128)(2,1)}) %reduce-scatter.55.cloned.1.call-update) | async-done | bytes 3472
  1256.0 14.2 %reduce-scatter.49.cloned.1.call-done = bf16[384,144]{1,0:T(8,128)(2,1)} async-done(((bf16[768,144]{1,0:T(8,128)(2,1)}), bf16[384,144]{1,0:T(8,128)(2,1)}) %reduce-scatter.49.cloned.1.call-update) | async-done | bytes 110608
  1271.9 23.2 %all-reduce.74.cloned.1.call-done = (bf16[1000,48]{0,1:T(8,128)(2,1)}, bf16[1000,48]{0,1:T(8,128)(2,1)}) async-done(((bf16[1000,48]{0,1:T(8,128)(2,1)}, bf16[1000,48]{0,1:T(8,128)(2,1)}), (bf16[1000,48]{0,1:T(8,128)(2,1)}, bf16[1000,48]{0,1:T(8,128)(2,1)})) %all-reduce.74.cloned.1.call-update) | async-done | bytes 192016
  1298.2 12.2 reduce-scatter.53.cloned.1.call-done
  1312.2 12.5 reduce-scatter.43.cloned.1.call-done
  1326.4 15.9 %reduce-scatter.45.cloned.1.call-done = bf16[384,288]{1,0:T(8,128)(2,1)} async-done(((bf16[768,288]{1,0:T(8,128)(2,1)}), bf16[384,288]{1,0:T(8,128)(2,1)}) %reduce-scatter.45.cloned.1.call-update) | async-done | bytes 221200
  (544 shorter events, 427.1 us)
Async XLA Ops:
  7.2 173.4 %all-gather.12.cloned.1.call-start = ((), (), s32[]{:S(2)}) async-start(), calls=%async_computation.14 | async-start | bytes 1671168 | tf_op jit(solution)/shard_map/all_gather | solution.py:151
  14.2 168.3 %all-gather.14.cloned.1.call-start = ((), (), s32[]{:S(2)}) async-start(), calls=%async_computation.15 | async-start | bytes 1671168 | tf_op jit(solution)/shard_map/all_gather | solution.py:152
  20.1 199.9 %all-gather.16.cloned.1.call-start = ((), (), s32[]{:S(2)}) async-start(), calls=%async_computation.16 | async-start | bytes 3760128 | tf_op jit(solution)/shard_map/all_gather | solution.py:154
  27.4 283.5 %all-gather.18.cloned.1.call-start = ((), (), s32[]{:S(2)}) async-start(), calls=%async_computation.17 | async-start | bytes 1253376 | tf_op jit(solution)/shard_map/all_gather | solution.py:155
  32.5 286.1 %all-gather.20.cloned.1.call-start = ((), (), s32[]{:S(2)}) async-start(), calls=%async_computation.18 | async-start | bytes 5013504 | tf_op jit(solution)/shard_map/all_gather | solution.py:156
  40.6 314.8 %all-gather.22.cloned.1.call-start = ((), (), s32[]{:S(2)}) async-start(), calls=%async_computation.19 | async-start | bytes 5013504 | tf_op jit(solution)/shard_map/all_gather | solution.py:157
  48.4 668.5 %all-gather.24.cloned.1.call-start = ((), (), s32[]{:S(2)}) async-start(), calls=%async_computation.20 | async-start | bytes 7520256 | tf_op jit(solution)/shard_map/all_gather | solution.py:172
  55.1 45.6 %collective-permute-start.8 = (bf16[768,288]{0,1:T(8,128)(2,1)S(1)}, bf16[768,288]{0,1:T(8,128)(2,1)S(1)}, u32[]{:S(2)}, u32[]{:S(2)}) collective-permute-start(bf16[768,288]{0,1:T(8,128)(2,1)S(1)} %all_gather.61), channel_id=1, source_target_pairs={{0,30},{2,0},{4,2},{6,4},{8,6},{10,8},{12,10},{14,12},{16,14},{18,... | collective-permute-start | bytes 1327112 | tf_op jit(solution)/shard_map/ppermute | solution.py:29
  55.1 44.4 %collective-permute-start = (bf16[768,288]{0,1:T(8,128)(2,1)S(1)}, bf16[768,288]{0,1:T(8,128)(2,1)S(1)}, u32[]{:S(2)}, u32[]{:S(2)}) collective-permute-start(bf16[768,288]{0,1:T(8,128)(2,1)S(1)} %all_gather.61), channel_id=1, source_target_pairs={{0,2},{2,4},{4,6},{6,8},{8,10},{10,12},{12,14},{14,16},{16,18},{18... | collective-permute-start | bytes 1327112 | tf_op jit(solution)/shard_map/ppermute | solution.py:26
  55.8 731.8 %reduce-scatter.37.cloned.1.call-start = ((), (), s32[]{:S(2)}) async-start(), calls=%async_computation.25 | async-start | bytes 1253376 | tf_op jit(solution)/shard_map/reduce_scatter | solution.py:344
  100.6 14.0 %collective-permute-start.9 = (bf16[768,288]{0,1:T(8,128)(2,1)S(1)}, bf16[768,288]{0,1:T(8,128)(2,1)S(1)}, u32[]{:S(2)}, u32[]{:S(2)}) collective-permute-start(bf16[768,288]{0,1:T(8,128)(2,1)S(1)} %collective-permute-done.8), channel_id=1, source_target_pairs={{0,30},{2,0},{4,2},{6,4},{8,6},{10,8},{12,10},{14,12},{16,14},{18,... | collective-permute-start | bytes 1327112 | tf_op jit(solution)/shard_map/ppermute | solution.py:29
  110.1 14.5 %collective-permute-start.2 = (bf16[768,288]{0,1:T(8,128)(2,1)S(1)}, bf16[768,288]{0,1:T(8,128)(2,1)S(1)}, u32[]{:S(2)}, u32[]{:S(2)}) collective-permute-start(bf16[768,288]{0,1:T(8,128)(2,1)S(1)} %collective-permute-done.1), channel_id=1, source_target_pairs={{0,2},{2,4},{4,6},{6,8},{8,10},{10,12},{12,14},{14,16},{16,18},{18... | collective-permute-start | bytes 1327112 | tf_op jit(solution)/shard_map/ppermute | solution.py:26
  124.6 14.4 %collective-permute-start.3 = (bf16[768,288]{0,1:T(8,128)(2,1)S(1)}, bf16[768,288]{0,1:T(8,128)(2,1)}, u32[]{:S(2)}, u32[]{:S(2)}) collective-permute-start(bf16[768,288]{0,1:T(8,128)(2,1)S(1)} %collective-permute-done.2), channel_id=1, source_target_pairs={{0,2},{2,4},{4,6},{6,8},{8,10},{10,12},{12,14},{14,16},{16,18},{18... | collective-permute-start | bytes 1327112 | tf_op jit(solution)/shard_map/ppermute | solution.py:26
  125.3 24.7 %collective-permute-start.11 = (bf16[768,288]{0,1:T(8,128)(2,1)}, bf16[768,288]{0,1:T(8,128)(2,1)}, u32[]{:S(2)}, u32[]{:S(2)}) collective-permute-start(bf16[768,288]{0,1:T(8,128)(2,1)} %collective-permute-done.10), channel_id=1, source_target_pairs={{0,30},{2,0},{4,2},{6,4},{8,6},{10,8},{12,10},{14,12},{16,14},{18,... | collective-permute-start | bytes 1327112 | tf_op jit(solution)/shard_map/ppermute | solution.py:29
  139.0 13.2 collective-permute-start.4
  152.1 12.3 collective-permute-start.5
  170.2 24.4 %collective-permute-start.14 = (bf16[768,288]{0,1:T(8,128)(2,1)}, bf16[768,288]{0,1:T(8,128)(2,1)}, u32[]{:S(2)}, u32[]{:S(2)}) collective-permute-start(bf16[768,288]{0,1:T(8,128)(2,1)} %collective-permute-done.13), channel_id=1, source_target_pairs={{0,30},{2,0},{4,2},{6,4},{8,6},{10,8},{12,10},{14,12},{16,14},{18,... | collective-permute-start | bytes 1327112 | tf_op jit(solution)/shard_map/ppermute | solution.py:29
  175.1 11.7 collective-permute-start.7
  593.6 195.8 %reduce-scatter.35.cloned.1.call-start = ((), (), s32[]{:S(2)}) async-start(), calls=%async_computation.24 | async-start | bytes 3760128 | tf_op jit(solution)/shard_map/reduce_scatter | solution.py:341
  680.6 130.7 %reduce-scatter.31.cloned.1.call-start = ((), (), s32[]{:S(2)}) async-start(), calls=%async_computation.22 | async-start | bytes 1671168 | tf_op jit(solution)/shard_map/reduce_scatter | solution.py:335
  723.8 150.7 %reduce-scatter.29.cloned.1.call-start = ((), (), s32[]{:S(2)}) async-start(), calls=%async_computation.21 | async-start | bytes 1671168 | tf_op jit(solution)/shard_map/reduce_scatter | solution.py:332
  726.5 226.3 %reduce-scatter.39.cloned.1.call-start = ((), (), s32[]{:S(2)}) async-start(), calls=%async_computation.26 | async-start | bytes 5013504 | tf_op jit(solution)/shard_map/reduce_scatter | solution.py:347
  739.0 292.8 %reduce-scatter.41.cloned.1.call-start = ((), (), s32[]{:S(2)}) async-start(), calls=%async_computation.27 | async-start | bytes 5013504 | tf_op jit(solution)/shard_map/reduce_scatter | solution.py:350
  750.1 374.7 %reduce-scatter.33.cloned.1.call-start = ((), (), s32[]{:S(2)}) async-start(), calls=%async_computation.23 | async-start | bytes 7520256 | tf_op jit(solution)/shard_map/reduce_scatter | solution.py:338
  755.2 427.1 %reduce-scatter.47.cloned.1.call-start = ((), (), s32[]{:S(2)}) async-start(), calls=%async_computation.30 | async-start | bytes 208896
  786.0 455.8 %reduce-scatter.55.cloned.1.call-start = ((), (), s32[]{:S(2)}) async-start(), calls=%async_computation.34 | async-start | bytes 835584
  787.5 466.8 %reduce-scatter.51.cloned.1.call-start = ((), (), s32[]{:S(2)}) async-start(), calls=%async_computation.32 | async-start | bytes 294912
  789.3 480.8 %reduce-scatter.49.cloned.1.call-start = ((), (), s32[]{:S(2)}) async-start(), calls=%async_computation.31 | async-start | bytes 589824
  791.3 503.8 %all-reduce.74.cloned.1.call-start = ((), (), s32[]{:S(2)}) async-start(), calls=%async_computation.35 | async-start | bytes 393216
  874.5 435.9 %reduce-scatter.53.cloned.1.call-start = ((), (), s32[]{:S(2)}) async-start(), calls=%async_computation.33 | async-start | bytes 589824
  954.7 370.0 %reduce-scatter.43.cloned.1.call-start = ((), (), s32[]{:S(2)}) async-start(), calls=%async_computation.28 | async-start | bytes 442368 | tf_op jit(solution)/shard_map/reduce_scatter | solution.py:379
  1031.8 310.5 %reduce-scatter.45.cloned.1.call-start = ((), (), s32[]{:S(2)}) async-start(), calls=%async_computation.29 | async-start | bytes 884736
  (141 other events, 3314.5 us)
Sparse Core Ops, SparseCore 0:
  14.3 41.4 all-gather.11
  58.6 38.9 all-gather.13
  99.9 61.1 all-gather.15
  163.2 40.0 all-gather.17
  205.5 52.2 all-gather.19
  259.9 51.9 all-gather.21
  314.1 65.1 all-gather.23
  593.7 58.6 reduce-scatter.36
  680.7 68.6 reduce-scatter.34
  752.9 58.2 reduce-scatter.30
  815.9 58.5 reduce-scatter.28
  878.2 74.5 reduce-scatter.38
  957.1 74.5 reduce-scatter.40
  1035.6 89.1 reduce-scatter.32
  1129.1 53.1 reduce-scatter.46
  1186.1 55.5 reduce-scatter.54
  1244.4 9.8 reduce-scatter.50
  1257.0 13.1 reduce-scatter.48
  1272.6 22.4 all-reduce.73
  1297.3 13.1 reduce-scatter.52
  1312.7 12.0 reduce-scatter.42
  1327.0 15.2 reduce-scatter.44
